TPU v7x, 32 devices: a whole 2x2x4 slice. The times are simulated.
32 devices in a mesh: src: 8 (over y, x, core), dst: 4 (over z).
Axes of the slice: x: 2, y: 2, z: 4, core: 2. Of those that a mesh axis runs over, the one named last changes fastest.
Arguments:
- raw: bfloat16 [4096, 256], P(('src', 'dst')), may hold values from -6 to 6
- enc_w1: bfloat16 [256, 512], replicated, may hold values from -0.375 to 0.375
- enc_w2: bfloat16 [512, 256], replicated, may hold values from -0.25 to 0.25
- block_weights: float32 [512, 128, 128], P(('src', 'dst')), may hold values from -0.125 to 0.125
- block_cols: int32 [512], P(('src', 'dst')), may hold values from 0 to 3, as said below
- noise: bfloat16 [3, 4096, 256], P(None, ('src', 'dst')), may hold values from -3 to 3
Outputs:
- encoded: bfloat16 [4096, 256], P(('src', 'dst'))
- hops: bfloat16 [3, 4096, 256], P(None, ('src', 'dst'))
Inputs may be any that keep to these rules, and one draw needn't show every extreme that they name: `block_cols`: entry b of each device's 16 entries belongs to row block b // 2; row blocks 2j and 2j+1 of a device together name every column block exactly once, each naming 4 // 2 distinct ones.
All inputs are finite; a program needn't handle non-finite values.
Results may differ from a plain program's by a relative error of at most 0.0058.
Values may be sent and summed in bfloat16 or wider, within the bound.
A program may use at most 128 MiB of HBM per device.

v0:
```python
import jax
import jax.numpy as jnp
from jax import lax
from jax.sharding import PartitionSpec as P

HOPS = 3


def normalize_rows(z):
    return (z * lax.rsqrt(jnp.mean(z * z, axis=-1, keepdims=True) + 1e-06)).astype(jnp.bfloat16)


def shards(raw, enc_w1, enc_w2, block_weights, block_cols, noise):
    hidden = jax.nn.silu(jnp.dot(raw, enc_w1, preferred_element_type=jnp.float32)).astype(
        jnp.bfloat16
    )
    encoded = normalize_rows(jnp.dot(hidden, enc_w2, preferred_element_type=jnp.float32))
    own_rows = raw.shape[0]
    block_side = block_weights.shape[1]
    width = encoded.shape[1]
    feats = encoded
    kept = []
    for step in range(HOPS):
        group = lax.all_gather(feats, "dst", axis=0, tiled=True)
        col_count = group.shape[0] // block_side
        half = col_count // 2
        col_blocks = group.astype(jnp.float32).reshape(col_count, block_side, width)
        fetched = jnp.take(col_blocks, block_cols, axis=0)
        prods = jnp.einsum("bij,bjw->biw", block_weights, fetched, precision=lax.Precision.HIGHEST)
        mine = lax.psum_scatter(
            prods.reshape(own_rows * lax.axis_size("src") // block_side, half, block_side, width)
            .sum(axis=1)
            .reshape(own_rows * lax.axis_size("src"), width),
            "src",
            scatter_dimension=0,
            tiled=True,
        )
        feats = normalize_rows(mine + noise[step].astype(jnp.float32))
        kept.append(feats)
    return (encoded, jnp.stack(kept))


def solution(mesh):
    placed = (
        P(("src", "dst"), None),
        P(),
        P(),
        P(("src", "dst"), None, None),
        P(("src", "dst")),
        P(None, ("src", "dst"), None),
    )
    return jax.shard_map(
        shards,
        mesh=mesh,
        in_specs=placed,
        out_specs=(P(("src", "dst"), None), P(None, ("src", "dst"), None)),
        check_vma=False,
    )
```

profile of v0, /device:TPU:0, one launch (start us, length us, event | category | flops | bytes accessed | tf_op | source)
XLA Modules:
  0.0 204.7 jit_solution(9608763618662152512)
XLA Ops:
  7.2 0.0 reduce-scatter.4.cloned.1.call-start
  7.2 0.7 compare_and_fusion
  8.0 0.7 compare_select_fusion
  8.6 1.5 multiply_reduce_fusion.3
  10.1 0.1 multiply_convert_fusion.4
  10.2 15.7 %all_gather.9 = bf16[512,256]{1,0:T(8,128)(2,1)S(1)} all-gather(bf16[128,256]{1,0:T(8,128)(2,1)S(1)} %multiply_convert_fusion.4), channel_id=1, replica_groups=mesh['src'=8,'dst'=4] {'dst'}, dimensions={0}, use_global_device_ids=true | all-gather | bytes 327680 | tf_op jit(solution)/shard_map/all_gather | solution.py:24
  25.9 2.0 gather_fusion
  28.0 5.4 %bitcast_reduce_fusion.2 = f32[8,128,256]{1,2,0:T(8,128)S(1)} fusion(f32[16,128,128]{2,1,0:T(8,128)S(1)} %copy-done, f32[16,128,256]{2,1,0:T(8,128)} %gather_fusion, pred[16]{0:T(512)(128)(4,1)S(1)} %compare_and_fusion), kind=kOutput, calls=%fused_computation.5 | convolution fusion | flops 806092800 | bytes 4194320 | tf_op jit(solution)/shard_map/bij,bjw->biw/dot_general | solution.py:29
  33.4 1.3 copy.15
  34.8 0.0 reduce-scatter.4.cloned.1.call-update
  34.8 0.0 reduce-scatter.6.cloned.1.call-start
  34.9 37.6 %reduce-scatter.4.cloned.1.call-done = f32[128,256]{1,0:T(8,128)} async-done(((f32[1024,256]{1,0:T(8,128)}), f32[128,256]{1,0:T(8,128)}) %reduce-scatter.4.cloned.1.call-update) | async-done | bytes 131088 | tf_op jit(solution)/shard_map/reduce_scatter | solution.py:30
  72.4 1.0 multiply_reduce_fusion.2
  73.5 1.0 multiply_convert_fusion.3
  74.5 13.8 %all_gather.10 = bf16[512,256]{1,0:T(8,128)(2,1)S(1)} all-gather(bf16[128,256]{1,0:T(8,128)(2,1)S(1)} %multiply_convert_fusion.3), channel_id=1, replica_groups=mesh['src'=8,'dst'=4] {'dst'}, dimensions={0}, use_global_device_ids=true | all-gather | bytes 327680 | tf_op jit(solution)/shard_map/all_gather | solution.py:24
  88.3 2.0 gather_fusion.1
  90.4 5.4 %bitcast_reduce_fusion.1 = f32[8,128,256]{1,2,0:T(8,128)S(1)} fusion(f32[16,128,128]{2,1,0:T(8,128)S(1)} %copy-done, f32[16,128,256]{2,1,0:T(8,128)} %gather_fusion.1, pred[16]{0:T(512)(128)(4,1)S(1)} %compare_and_fusion), kind=kOutput, calls=%fused_computation.4 | convolution fusion | flops 806092800 | bytes 4194320 | tf_op jit(solution)/shard_map/bij,bjw->biw/dot_general | solution.py:29
  95.8 1.3 copy.17
  97.2 0.0 reduce-scatter.6.cloned.1.call-update
  97.2 0.0 reduce-scatter.8.cloned.1.call-start
  97.2 36.7 %reduce-scatter.6.cloned.1.call-done = f32[128,256]{1,0:T(8,128)} async-done(((f32[1024,256]{1,0:T(8,128)}), f32[128,256]{1,0:T(8,128)}) %reduce-scatter.6.cloned.1.call-update) | async-done | bytes 131088 | tf_op jit(solution)/shard_map/reduce_scatter | solution.py:30
  133.9 1.0 multiply_reduce_fusion.1
  134.9 1.0 multiply_convert_fusion.2
  135.9 14.1 %all_gather.11 = bf16[512,256]{1,0:T(8,128)(2,1)S(1)} all-gather(bf16[128,256]{1,0:T(8,128)(2,1)S(1)} %multiply_convert_fusion.2), channel_id=1, replica_groups=mesh['src'=8,'dst'=4] {'dst'}, dimensions={0}, use_global_device_ids=true | all-gather | bytes 327680 | tf_op jit(solution)/shard_map/all_gather | solution.py:24
  150.0 2.0 gather_fusion.2
  152.1 5.4 %bitcast_reduce_fusion = f32[8,128,256]{1,2,0:T(8,128)S(1)} fusion(f32[16,128,128]{2,1,0:T(8,128)S(1)} %copy-done, f32[16,128,256]{2,1,0:T(8,128)} %gather_fusion.2, pred[16]{0:T(512)(128)(4,1)S(1)} %compare_and_fusion), kind=kOutput, calls=%fused_computation.3 | convolution fusion | flops 806092800 | bytes 4194320 | tf_op jit(solution)/shard_map/bij,bjw->biw/dot_general | solution.py:29
  157.5 1.3 copy.19
  158.8 0.0 reduce-scatter.8.cloned.1.call-update
  158.9 36.6 %reduce-scatter.8.cloned.1.call-done = f32[128,256]{1,0:T(8,128)} async-done(((f32[1024,256]{1,0:T(8,128)}), f32[128,256]{1,0:T(8,128)}) %reduce-scatter.8.cloned.1.call-update) | async-done | bytes 131088 | tf_op jit(solution)/shard_map/reduce_scatter | solution.py:30
  195.5 1.0 multiply_reduce_fusion
  196.5 1.0 fusion.19
  197.5 0.7 pad_maximum_fusion
  (14 shorter events, 0.2 us)
Async XLA Ops:
  7.2 20.8 %copy-start = (f32[16,128,128]{2,1,0:T(8,128)S(1)}, f32[16,128,128]{2,1,0:T(8,128)}, u32[]{:S(2)}) copy-start(f32[16,128,128]{2,1,0:T(8,128)} %param.11) | copy-start | bytes 3145732
  7.2 65.3 %reduce-scatter.4.cloned.1.call-start = ((), (), s32[]{:S(2)}) async-start(), calls=%async_computation.3 | async-start | bytes 1179648 | tf_op jit(solution)/shard_map/reduce_scatter | solution.py:30
  10.2 17.7 %copy-start.2 = (bf16[128,256]{1,0:T(8,128)(2,1)}, bf16[128,256]{1,0:T(8,128)(2,1)S(1)}, u32[]{:S(2)}) copy-start(bf16[128,256]{1,0:T(8,128)(2,1)S(1)} %multiply_convert_fusion.4) | copy-start | bytes 196612
  33.4 39.0 %copy-start.1 = (bf16[3,128,256]{2,1,0:T(8,128)(2,1)S(1)}, bf16[3,128,256]{2,1,0:T(8,128)(2,1)}, u32[]{:S(2)}) copy-start(bf16[3,128,256]{2,1,0:T(8,128)(2,1)} %param.13) | copy-start | bytes 589828
  34.8 99.1 %reduce-scatter.6.cloned.1.call-start = ((), (), s32[]{:S(2)}) async-start(), calls=%async_computation.4 | async-start | bytes 1179648 | tf_op jit(solution)/shard_map/reduce_scatter | solution.py:30
  97.2 98.3 %reduce-scatter.8.cloned.1.call-start = ((), (), s32[]{:S(2)}) async-start(), calls=%async_computation.5 | async-start | bytes 1179648 | tf_op jit(solution)/shard_map/reduce_scatter | solution.py:30
Sparse Core Ops, SparseCore 0:
  34.9 37.4 reduce-scatter.3
  97.3 36.5 reduce-scatter.5
  159.0 36.4 reduce-scatter.7
where the time goes:
time: 205 us
  waiting for transfers between devices  111 us (54%)
  blocking collectives  43.6 us (21%)
  matrix products  17.8 us (9%)
  between operations  13.9 us (7%)
  local copies, waits for them, and re-layouts  10.1 us (5%)
  other arithmetic  8.34 us (4%)
    reduce_scatter x3, waiting for transfers between devices, shards(): lax.psum_scatter(prods.reshape(own_rows * lax.axis_size('src') // block_s...  111 us
    all_gather x3, blocking collectives, shards(): group = lax.all_gather(feats, 'dst', axis=0, tiled=True)  43.6 us
    dot_general x3, matrix products, shards(): jnp.einsum('bij,bjw->biw', block_weights, fetched, precision=lax.Precisio...  16.3 us
    gather x3, local copies, waits for them, and re-layouts, shards(): fetched = jnp.take(col_blocks, block_cols, axis=0)  6.1 us
  transfers between devices with their start and end apart: 3, of which 3 were waited for; matrix products, arithmetic and copies ran while one was open for 0% of the time, Pallas kernels for 0%

commit v1 on v0

v1 whole, which is shorter than its diff:
```python
import functools

import jax
import jax.numpy as jnp
from jax import lax
from jax.experimental import pallas as pl
from jax.experimental.pallas import tpu as pltpu
from jax.sharding import PartitionSpec as P

MESH = pl.DeviceIdType.MESH
CHUNKS = 2
F32 = jnp.float32
BF16 = jnp.bfloat16


def shifted(me, step, count):
    if count & (count - 1) == 0:
        return me ^ step, me ^ step
    return lax.rem(me + step, count), lax.rem(me + count - step, count)


def kernel(
    n_src, n_dst, hops,
    raw_h, w1_h, w2_h, bw_h, cols, noise_h,
    enc_h, hops_h,
    raw_v, w1_v, w2_v, bw_v, noise_v, enc_v, hops_v, wcat, gath, out1, in1, out2, in2, acc,
    load_sem, store_sem, g_send, g_recv, send1, recv1, send2, recv2,
):
    src, dst = lax.axis_index("src"), lax.axis_index("dst")
    pairs = n_src // 2
    pair, core = src // 2, lax.rem(src, 2)
    partner = pair * 2 + 1 - core
    side = bw_v.shape[1]
    per_row = bw_v.shape[0] // n_src
    width = enc_v.shape[1]
    part = width // CHUNKS

    loads = [
        pltpu.make_async_copy(a, b, load_sem.at[i])
        for i, (a, b) in enumerate(
            ((raw_h, raw_v), (w1_h, w1_v), (w2_h, w2_v), (bw_h, bw_v), (noise_h, noise_v))
        )
    ]
    for load in loads:
        load.start()

    barrier = pltpu.get_barrier_semaphore()
    greeted = 0
    for step in range(1, n_dst):
        to, _ = shifted(dst, step, n_dst)
        pl.semaphore_signal(barrier, inc=1, device_id={"dst": to}, device_id_type=MESH)
        greeted += 1
    for step in range(1, pairs):
        to, _ = shifted(pair, step, pairs)
        pl.semaphore_signal(barrier, inc=1, device_id={"src": to * 2 + core}, device_id_type=MESH)
        greeted += 1
    pl.semaphore_signal(barrier, inc=1, device_id={"src": partner}, device_id_type=MESH)
    greeted += 1

    def normalized(z):
        scale = lax.rsqrt(jnp.sum(z * z, axis=-1, keepdims=True) * (1.0 / width) + 1e-06)
        return (z * scale).astype(BF16)

    loads[0].wait()
    loads[1].wait()
    v = jnp.dot(raw_v[...], w1_v[...], preferred_element_type=F32)
    hidden = (v * jax.nn.sigmoid(v)).astype(BF16)
    loads[2].wait()
    feats = normalized(jnp.dot(hidden, w2_v[...], preferred_element_type=F32))
    enc_v[...] = feats
    stores = [pltpu.make_async_copy(enc_v, enc_h, store_sem.at[0])]
    stores[0].start()

    pl.semaphore_wait(barrier, greeted)
    sent = []

    def gather(hop, feats):
        waits = []
        for c in range(CHUNKS):
            gath[hop][c][dst] = feats[:, c * part : (c + 1) * part]
        for c in range(CHUNKS):
            buf = gath[hop][c]
            mine = []
            for step in reversed(range(1, n_dst)):
                to, _ = shifted(dst, step, n_dst)
                copy = pltpu.make_async_remote_copy(
                    src_ref=buf.at[dst],
                    dst_ref=buf.at[dst],
                    send_sem=g_send.at[hop, c, step - 1],
                    recv_sem=g_recv.at[hop, c, step - 1],
                    device_id={"dst": to},
                    device_id_type=MESH,
                )
                copy.start()
                mine.append(copy)
            waits.append(mine)
            sent.extend(mine)
        return waits

    waits = gather(0, feats)

    loads[3].wait()
    for b in range(bw_v.shape[0]):
        r, i = divmod(b, per_row)
        w = bw_v[b]
        high = w.astype(BF16)
        wcat[r, 0:side, i * side : (i + 1) * side] = high
        wcat[r, side : 2 * side, i * side : (i + 1) * side] = (w - high.astype(F32)).astype(BF16)
    loads[4].wait()

    order = list(reversed(range(pairs)))
    for hop in range(hops):
        arrivals = []
        for c in range(CHUNKS):
            buf = gath[hop][c]
            for copy in waits[c]:
                copy.wait_recv()

            def product(row):
                picked = [buf[cols[row * per_row + i]] for i in range(per_row)]
                both = jnp.dot(
                    wcat[row], jnp.concatenate(picked, axis=0), preferred_element_type=F32
                )
                return both[:side] + both[side:]

            first = {}
            for step in order:
                to, _ = shifted(pair, step, pairs) if step else (pair, pair)
                out1[hop, c, step] = product(to * 2 + 1 - core).astype(BF16)
                copy = pltpu.make_async_remote_copy(
                    src_ref=out1.at[hop, c, step],
                    dst_ref=in1.at[hop, c, step],
                    send_sem=send1.at[hop, c, step],
                    recv_sem=recv1.at[hop, c, step],
                    device_id={"src": partner},
                    device_id_type=MESH,
                )
                copy.start()
                first[step] = copy
                sent.append(copy)
            second = []
            for step in order:
                to, _ = shifted(pair, step, pairs) if step else (pair, pair)
                mine = product(to * 2 + core)
                first[step].wait_recv()
                mine = mine + in1[hop, c, step].astype(F32)
                if step == 0:
                    acc[c] = mine
                    continue
                out2[hop, c, step - 1] = mine.astype(BF16)
                copy = pltpu.make_async_remote_copy(
                    src_ref=out2.at[hop, c, step - 1],
                    dst_ref=in2.at[hop, c, step - 1],
                    send_sem=send2.at[hop, c, step - 1],
                    recv_sem=recv2.at[hop, c, step - 1],
                    device_id={"src": to * 2 + core},
                    device_id_type=MESH,
                )
                copy.start()
                second.append(copy)
                sent.append(copy)
            arrivals.append(second)
        sums = []
        for c in range(CHUNKS):
            z = acc[c] + noise_v[hop, :, c * part : (c + 1) * part].astype(F32)
            for copy in arrivals[c]:
                copy.wait_recv()
            for step in range(1, pairs):
                z = z + in2[hop, c, step - 1].astype(F32)
            sums.append(z)
        feats = normalized(jnp.concatenate(sums, axis=1) if CHUNKS > 1 else sums[0])
        if hop < hops - 1:
            waits = gather(hop + 1, feats)
        hops_v[hop] = feats
        store = pltpu.make_async_copy(hops_v.at[hop], hops_h.at[hop], store_sem.at[hop + 1])
        store.start()
        stores.append(store)
    for copy in sent:
        copy.wait_send()
    for store in stores:
        store.wait()


def shards(n_src, n_dst, raw, enc_w1, enc_w2, block_weights, block_cols, noise):
    blocks, side, _ = block_weights.shape
    hops, rows, width = noise.shape
    pairs = n_src // 2
    per_row = blocks // n_src
    part = width // CHUNKS
    assert rows == side and n_src % 2 == 0
    anywhere = pl.BlockSpec(memory_space=pl.ANY)
    dma = pltpu.SemaphoreType.DMA
    far = max(pairs - 1, 1)
    near = max(n_dst - 1, 1)
    return pl.pallas_call(
        functools.partial(kernel, n_src, n_dst, hops),
        out_shape=(
            jax.ShapeDtypeStruct((rows, width), BF16),
            jax.ShapeDtypeStruct((hops, rows, width), BF16),
        ),
        in_specs=[anywhere] * 4 + [pl.BlockSpec(memory_space=pltpu.SMEM), anywhere],
        out_specs=(anywhere, anywhere),
        scratch_shapes=[
            pltpu.VMEM(raw.shape, BF16),
            pltpu.VMEM(enc_w1.shape, BF16),
            pltpu.VMEM(enc_w2.shape, BF16),
            pltpu.VMEM(block_weights.shape, F32),
            pltpu.VMEM(noise.shape, BF16),
            pltpu.VMEM((rows, width), BF16),
            pltpu.VMEM((hops, rows, width), BF16),
            pltpu.VMEM((n_src, 2 * side, per_row * side), BF16),
            [[pltpu.VMEM((n_dst, rows, part), BF16) for _ in range(CHUNKS)] for _ in range(hops)],
            pltpu.VMEM((hops, CHUNKS, pairs, rows, part), BF16),
            pltpu.VMEM((hops, CHUNKS, pairs, rows, part), BF16),
            pltpu.VMEM((hops, CHUNKS, far, rows, part), BF16),
            pltpu.VMEM((hops, CHUNKS, far, rows, part), BF16),
            pltpu.VMEM((CHUNKS, rows, part), F32),
            dma((5,)),
            dma((hops + 1,)),
            dma((hops, CHUNKS, near)),
            dma((hops, CHUNKS, near)),
            dma((hops, CHUNKS, pairs)),
            dma((hops, CHUNKS, pairs)),
            dma((hops, CHUNKS, far)),
            dma((hops, CHUNKS, far)),
        ],
        compiler_params=pltpu.CompilerParams(
            collective_id=0, has_side_effects=True, vmem_limit_bytes=60 * 1024 * 1024
        ),
    )(raw, enc_w1, enc_w2, block_weights, block_cols, noise)


def solution(mesh):
    placed = (
        P(("src", "dst"), None),
        P(),
        P(),
        P(("src", "dst"), None, None),
        P(("src", "dst")),
        P(None, ("src", "dst"), None),
    )
    return jax.shard_map(
        functools.partial(shards, mesh.shape["src"], mesh.shape["dst"]),
        mesh=mesh,
        in_specs=placed,
        out_specs=(P(("src", "dst"), None), P(None, ("src", "dst"), None)),
        check_vma=False,
    )
```

time: 205 us -> 49.6 us (0.24)
  waiting for transfers between devices: 111 us -> 0 us
  Pallas kernels: 0 us -> 45.7 us
  blocking collectives: 43.6 us -> 0 us
  matrix products: 17.8 us -> 0 us
  between operations: 13.9 us -> 0.64 us
  other arithmetic: 8.34 us -> 0 us
  local copies, waits for them, and re-layouts: 10.1 us -> 3.09 us
    reduce_scatter x3 -> x0, waiting for transfers between devices: 111 us -> none  [shards(): lax.psum_scatter(prods.reshape(own_rows * lax.axis_size('src') // block_s...]
    pallas_call x0 -> x1, Pallas kernels: none -> 45.7 us  [shards(): pl.pallas_call(functools.partial(kernel, n_src, n_dst, hops), out_shape=(...]
    all_gather x3 -> x0, blocking collectives: 43.6 us -> none  [shards(): group = lax.all_gather(feats, 'dst', axis=0, tiled=True)]
    dot_general x4 -> x0, matrix products: 17.8 us -> none  [the longest x3 16.3 us: shards(): jnp.einsum('bij,bjw->biw', block_weights, fetched, precision=lax.Precisio...]
    gather x3 -> x0, local copies, waits for them, and re-layouts: 6.1 us -> none  [shards(): fetched = jnp.take(col_blocks, block_cols, axis=0)]
    reduce_sum x3 -> x0, local copies, waits for them, and re-layouts: 3.98 us -> none  [shards(): mine = lax.psum_scatter(prods.reshape(own_rows * lax.axis_size('src') //...]
    unnamed x6 -> x2, local copies, waits for them, and re-layouts: 0.02 us -> 3.09 us
    reduce_sum x3 -> x0, other arithmetic: 3.02 us -> none  [normalize_rows(): jnp.mean(z * z, axis=-1, keepdims=True) + 1e-06]
  transfers between devices with their start and end apart: 3 -> 0, of which waited for: 3 -> 0; matrix products, arithmetic and copies ran while one was open for 0% -> 0% of each run, Pallas kernels for 0% -> 0%
where the time goes in v1:
time: 49.6 us; the launch traced here: 49.4 us
  Pallas kernels  45.7 us (92%)
  local copies, waits for them, and re-layouts  3.09 us (6%)
  between operations  0.64 us (1%)
    pallas_call x1, Pallas kernels, shards(): pl.pallas_call(functools.partial(kernel, n_src, n_dst, hops), out_shape=(...  45.7 us
    unnamed x2, local copies, waits for them, and re-layouts  3.09 us

profile of v1, /device:TPU:0, one launch (start us, length us, event | category | flops | bytes accessed | tf_op | source)
XLA Modules:
  0.0 49.4 jit_solution(7236720249596477445)
XLA Ops:
  0.6 45.7 %shard_map.77 = (bf16[128,256]{1,0:T(8,128)(2,1)}, bf16[3,128,256]{2,1,0:T(8,128)(2,1)}) custom-call(bf16[128,256]{1,0:T(8,128)(2,1)} %raw_h.1, bf16[256,512]{1,0:T(8,128)(2,1)} %w1_h.1, bf16[512,256]{1,0:T(8,128)(2,1)} %w2_h.1, f32[16,128,128]{2,1,0:T(8,128)} %bw_h.1, s32[16]{0:T(128)} %cols.1, bf16[3,128,256]{2,1,0:T(8,128)(2,1)} %noise_h.1), custom_call_target="tpu_custom_call" | custom-call | tf_op jit(solution)/shard_map/pallas_call | solution.py:195
  46.3 1.5 %copy.10 = bf16[128,256]{1,0:T(8,128)(2,1)} copy(bf16[128,256]{1,0:T(8,128)(2,1)} %get-tuple-element.4) | data formatting | bytes 131072
  47.8 1.6 %copy.11 = bf16[3,128,256]{2,1,0:T(8,128)(2,1)} copy(bf16[3,128,256]{2,1,0:T(8,128)(2,1)} %get-tuple-element.5) | data formatting | bytes 393216

commit v2 on v1

--- a/solution.py
+++ b/solution.py
@@ -35,15 +35,6 @@
     width = enc_v.shape[1]
     part = width // CHUNKS
 
-    loads = [
-        pltpu.make_async_copy(a, b, load_sem.at[i])
-        for i, (a, b) in enumerate(
-            ((raw_h, raw_v), (w1_h, w1_v), (w2_h, w2_v), (bw_h, bw_v), (noise_h, noise_v))
-        )
-    ]
-    for load in loads:
-        load.start()
-
     barrier = pltpu.get_barrier_semaphore()
     greeted = 0
     for step in range(1, n_dst):
@@ -57,6 +48,15 @@
     pl.semaphore_signal(barrier, inc=1, device_id={"src": partner}, device_id_type=MESH)
     greeted += 1
 
+    loads = [
+        pltpu.make_async_copy(a, b, load_sem.at[i])
+        for i, (a, b) in enumerate(
+            ((raw_h, raw_v), (w1_h, w1_v), (w2_h, w2_v), (bw_h, bw_v), (noise_h, noise_v))
+        )
+    ]
+    for load in loads:
+        load.start()
+
     def normalized(z):
         scale = lax.rsqrt(jnp.sum(z * z, axis=-1, keepdims=True) * (1.0 / width) + 1e-06)
         return (z * scale).astype(BF16)
@@ -81,7 +81,7 @@
         for c in range(CHUNKS):
             buf = gath[hop][c]
             mine = []
-            for step in reversed(range(1, n_dst)):
+            for step in range(1, n_dst):
                 to, _ = shifted(dst, step, n_dst)
                 copy = pltpu.make_async_remote_copy(
                     src_ref=buf.at[dst],
@@ -181,6 +181,24 @@
         store.wait()
 
 
+def finish(enc_i, hops_i, enc_o, hops_o, enc_v, hops_v, sem):
+    reads = [
+        pltpu.make_async_copy(hops_i, hops_v, sem.at[0]),
+        pltpu.make_async_copy(enc_i, enc_v, sem.at[1]),
+    ]
+    writes = [
+        pltpu.make_async_copy(hops_v, hops_o, sem.at[2]),
+        pltpu.make_async_copy(enc_v, enc_o, sem.at[3]),
+    ]
+    for read in reads:
+        read.start()
+    for read, write in zip(reads, writes):
+        read.wait()
+        write.start()
+    for write in writes:
+        write.wait()
+
+
 def shards(n_src, n_dst, raw, enc_w1, enc_w2, block_weights, block_cols, noise):
     blocks, side, _ = block_weights.shape
     hops, rows, width = noise.shape
@@ -192,7 +210,7 @@
     dma = pltpu.SemaphoreType.DMA
     far = max(pairs - 1, 1)
     near = max(n_dst - 1, 1)
-    return pl.pallas_call(
+    encoded, kept = pl.pallas_call(
         functools.partial(kernel, n_src, n_dst, hops),
         out_shape=(
             jax.ShapeDtypeStruct((rows, width), BF16),
@@ -228,6 +246,17 @@
             collective_id=0, has_side_effects=True, vmem_limit_bytes=60 * 1024 * 1024
         ),
     )(raw, enc_w1, enc_w2, block_weights, block_cols, noise)
+    shapes = (
+        jax.ShapeDtypeStruct((rows, width), BF16),
+        jax.ShapeDtypeStruct((hops, rows, width), BF16),
+    )
+    return pl.pallas_call(
+        finish,
+        out_shape=shapes,
+        in_specs=[anywhere, anywhere],
+        out_specs=(anywhere, anywhere),
+        scratch_shapes=[pltpu.VMEM(s.shape, BF16) for s in shapes] + [dma((4,))],
+    )(encoded, kept)
 
 
 def solution(mesh):

time: 49.6 us -> 47.2 us (0.952)
  local copies, waits for them, and re-layouts: 3.09 us -> 0 us
  Pallas kernels: 45.7 us -> 46.4 us
    unnamed x2 -> x0, local copies, waits for them, and re-layouts: 3.09 us -> none
    pallas_call x0 -> x1, Pallas kernels: none -> 1.66 us  [shards(): pl.pallas_call(finish, out_shape=shapes, in_specs=[anywhere, anywhere], o...]
    pallas_call x1, Pallas kernels: 45.7 us -> 44.8 us  [shards(): pl.pallas_call(functools.partial(kernel, n_src, n_dst, hops), out_shape=(...]
where the time goes in v2:
time: 47.2 us; the launch traced here: 47.1 us
  Pallas kernels  46.4 us (98%)
  between operations  0.64 us (1%)
    pallas_call x1, Pallas kernels, shards(): pl.pallas_call(functools.partial(kernel, n_src, n_dst, hops), out_shape=(...  44.8 us
    pallas_call x1, Pallas kernels, shards(): pl.pallas_call(finish, out_shape=shapes, in_specs=[anywhere, anywhere], o...  1.66 us

profile of v2, /device:TPU:0, one launch (start us, length us, event | category | flops | bytes accessed | tf_op | source)
XLA Modules:
  0.0 47.1 jit_solution(3895513405010158063)
XLA Ops:
  0.6 44.8 %shard_map.77 = (bf16[128,256]{1,0:T(8,128)(2,1)}, bf16[3,128,256]{2,1,0:T(8,128)(2,1)}) custom-call(bf16[128,256]{1,0:T(8,128)(2,1)} %raw_h.1, bf16[256,512]{1,0:T(8,128)(2,1)} %w1_h.1, bf16[512,256]{1,0:T(8,128)(2,1)} %w2_h.1, f32[16,128,128]{2,1,0:T(8,128)} %bw_h.1, s32[16]{0:T(128)} %cols.1, bf16[3,128,256]{2,1,0:T(8,128)(2,1)} %noise_h.1), custom_call_target="tpu_custom_call" | custom-call | tf_op jit(solution)/shard_map/pallas_call | solution.py:213
  45.4 1.7 %shard_map.78 = (bf16[128,256]{1,0:T(8,128)(2,1)}, bf16[3,128,256]{2,1,0:T(8,128)(2,1)}) custom-call(bf16[128,256]{1,0:T(8,128)(2,1)} %get-tuple-element.4.enc_i, bf16[3,128,256]{2,1,0:T(8,128)(2,1)} %get-tuple-element.5.hops_i), custom_call_target="tpu_custom_call" | custom-call | tf_op jit(solution)/shard_map/pallas_call | solution.py:253

commit v3 on v2

--- a/solution.py
+++ b/solution.py
@@ -109,6 +109,17 @@
     loads[4].wait()
 
     order = list(reversed(range(pairs)))
+    def at(step):
+        return shifted(pair, step, pairs)[0] if step else pair
+
+    named = {
+        (step, side_core): [
+            cols[(at(step) * 2 + (core if side_core else 1 - core)) * per_row + i]
+            for i in range(per_row)
+        ]
+        for step in order
+        for side_core in (0, 1)
+    }
     for hop in range(hops):
         arrivals = []
         for c in range(CHUNKS):
@@ -116,8 +127,8 @@
             for copy in waits[c]:
                 copy.wait_recv()
 
-            def product(row):
-                picked = [buf[cols[row * per_row + i]] for i in range(per_row)]
+            def product(row, step, own):
+                picked = [buf[name] for name in named[step, own]]
                 both = jnp.dot(
                     wcat[row], jnp.concatenate(picked, axis=0), preferred_element_type=F32
                 )
@@ -126,7 +137,7 @@
             first = {}
             for step in order:
                 to, _ = shifted(pair, step, pairs) if step else (pair, pair)
-                out1[hop, c, step] = product(to * 2 + 1 - core).astype(BF16)
+                out1[hop, c, step] = product(to * 2 + 1 - core, step, 0).astype(BF16)
                 copy = pltpu.make_async_remote_copy(
                     src_ref=out1.at[hop, c, step],
                     dst_ref=in1.at[hop, c, step],
@@ -141,7 +152,7 @@
             second = []
             for step in order:
                 to, _ = shifted(pair, step, pairs) if step else (pair, pair)
-                mine = product(to * 2 + core)
+                mine = product(to * 2 + core, step, 1)
                 first[step].wait_recv()
                 mine = mine + in1[hop, c, step].astype(F32)
                 if step == 0:
@@ -163,9 +174,8 @@
         sums = []
         for c in range(CHUNKS):
             z = acc[c] + noise_v[hop, :, c * part : (c + 1) * part].astype(F32)
-            for copy in arrivals[c]:
-                copy.wait_recv()
             for step in range(1, pairs):
+                arrivals[c][pairs - 1 - step].wait_recv()
                 z = z + in2[hop, c, step - 1].astype(F32)
             sums.append(z)
         feats = normalized(jnp.concatenate(sums, axis=1) if CHUNKS > 1 else sums[0])

time: 47.2 us -> 47.1 us (level)
  no operation moved by 1% of the time
where the time goes in v3:
time: 47.1 us; the launch traced here: 46.9 us
  Pallas kernels  46.3 us (98%)
  between operations  0.64 us (1%)
    pallas_call x1, Pallas kernels, shards(): pl.pallas_call(functools.partial(kernel, n_src, n_dst, hops), out_shape=(...  44.6 us
    pallas_call x1, Pallas kernels, shards(): pl.pallas_call(finish, out_shape=shapes, in_specs=[anywhere, anywhere], o...  1.66 us

profile of v3, /device:TPU:0, one launch (start us, length us, event | category | flops | bytes accessed | tf_op | source)
XLA Modules:
  0.0 46.9 jit_solution(9458505884699949569)
XLA Ops:
  0.6 44.6 %shard_map.77 = (bf16[128,256]{1,0:T(8,128)(2,1)}, bf16[3,128,256]{2,1,0:T(8,128)(2,1)}) custom-call(bf16[128,256]{1,0:T(8,128)(2,1)} %raw_h.1, bf16[256,512]{1,0:T(8,128)(2,1)} %w1_h.1, bf16[512,256]{1,0:T(8,128)(2,1)} %w2_h.1, f32[16,128,128]{2,1,0:T(8,128)} %bw_h.1, s32[16]{0:T(128)} %cols.1, bf16[3,128,256]{2,1,0:T(8,128)(2,1)} %noise_h.1), custom_call_target="tpu_custom_call" | custom-call | tf_op jit(solution)/shard_map/pallas_call | solution.py:223
  45.3 1.7 %shard_map.78 = (bf16[128,256]{1,0:T(8,128)(2,1)}, bf16[3,128,256]{2,1,0:T(8,128)(2,1)}) custom-call(bf16[128,256]{1,0:T(8,128)(2,1)} %get-tuple-element.4.enc_i, bf16[3,128,256]{2,1,0:T(8,128)(2,1)} %get-tuple-element.5.hops_i), custom_call_target="tpu_custom_call" | custom-call | tf_op jit(solution)/shard_map/pallas_call | solution.py:263
